TPU v7x, 32 devices: a whole 2x2x4 slice. The times are simulated.
32 devices in a mesh: groups: 2 (over x), tensor: 4 (over y, core), dp: 4 (over z).
Axes of the slice: x: 2, y: 2, z: 4, core: 2. Of those that a mesh axis runs over, the one named last changes fastest.
Arguments:
- hidden_in: bfloat16 [1024, 8192], P(('groups', 'dp'), 'tensor'), parts along dimension 0, may hold values from -6 to 6
- out_grad: bfloat16 [1024, 8192], P(('groups', 'dp'), 'tensor'), parts along dimension 0, may hold values from -6 to 6
- w_gate_up: bfloat16 [2, 28672, 8192], P(None, ('tensor', 'dp')), may hold values from -0.0625 to 0.0625
- w_down: bfloat16 [28672, 8192], P(('tensor', 'dp')), may hold values from -0.03125 to 0.03125
- feat_proj: bfloat16 [8192, 192], P('tensor'), may hold values from -0.0625 to 0.0625
- unit_proj: bfloat16 [28672, 192], P(('tensor', 'dp')), may hold values from -0.03125 to 0.03125
- precond: float32 [3, 4096, 4096], P(None, ('tensor', 'dp')), may hold values from -20 to 20
Outputs:
- precond_grad: float32 [3, 8, 4096], P(None, 'groups', ('tensor', 'dp')), parts along dimension 1
There are 2 independent parts, one for each index of `groups`. A program takes and returns all parts, laid end to end along the dimension named above; an argument that names none is the same for every part. Nothing has to cross between parts.
All inputs are finite; a program needn't handle non-finite values.
Results may differ from a plain program's by a relative error of at most 0.0029.
Values may be sent and summed in bfloat16 or wider, within the bound.
No kernel may reach another device: no remote copies, remote signals or barrier semaphores. Data moves between devices by JAX's collectives and lax.ppermute only.
A program may use at most 256 MiB of HBM per device.

v0:
```python
import jax
import jax.numpy as jnp
from jax import lax
from jax.sharding import PartitionSpec as P

K = 64
SEQ = 128
contract_last = (((1,), (1,)), ((), ()))


def project_pair(rows_in, rows_out, columns):
    return jnp.concatenate(
        [
            jnp.dot(rows_in, columns[:, : 2 * K], preferred_element_type=jnp.float32),
            jnp.dot(rows_out, columns[:, 2 * K :], preferred_element_type=jnp.float32),
        ],
        axis=1,
    )


def form_sketch(in_side, out_side):
    seq_count = in_side.shape[0] // SEQ
    left_rows = in_side.reshape(seq_count, SEQ, 3, K)
    right_rows = out_side.reshape(seq_count, SEQ, 3, K)
    sketch = jnp.einsum("stwi,stwj->wsij", left_rows, right_rows, precision=lax.Precision.HIGHEST)
    sketch = sketch * SEQ ** (-0.5)
    return sketch.reshape(3, seq_count, K * K)


def local(hidden_in, out_grad, w_gate_up, w_down, feat_proj, unit_proj, precond):
    unit_width = w_down.shape[0]
    model_width = w_down.shape[1]
    w_both = w_gate_up.reshape(2 * unit_width, model_width)
    paired = jnp.stack([hidden_in, out_grad])
    tokens = hidden_in.shape[0] * lax.axis_size("dp")
    columns = lax.all_gather(feat_proj, "tensor", axis=0, tiled=True)
    feat_side = None
    rows_all = lax.all_gather(paired, "dp", axis=1, tiled=True)
    initial = [
        jnp.zeros((tokens, 2 * unit_width), jnp.float32),
        jnp.zeros((tokens, unit_width), jnp.float32),
    ]
    initial.append(jnp.zeros((tokens, 3 * K), jnp.float32))
    pieces = lax.all_gather(rows_all, "tensor", axis=2, tiled=True)
    result = [
        lax.dot_general(pieces[0], w_both, contract_last, preferred_element_type=jnp.float32),
        lax.dot_general(pieces[1], w_down, contract_last, preferred_element_type=jnp.float32),
    ]
    result.append(project_pair(pieces[0], pieces[1], columns))
    folded = tuple(result)
    pre_act = folded[0]
    hid_grad = folded[1]
    feat_side = folded[2]
    gate_pre = pre_act[:, :unit_width]
    up_pre = pre_act[:, unit_width:]
    gate_sig = jax.nn.sigmoid(gate_pre)
    silu_gate = gate_pre * gate_sig
    hidden = (silu_gate * up_pre).astype(jnp.bfloat16)
    gate_grad = (hid_grad * up_pre * gate_sig * (1.0 + gate_pre * (1.0 - gate_sig))).astype(
        jnp.bfloat16
    )
    up_grad = (hid_grad * silu_gate).astype(jnp.bfloat16)
    unit_part = jnp.concatenate(
        [
            jnp.dot(gate_grad, unit_proj[:, :K], preferred_element_type=jnp.float32),
            jnp.dot(up_grad, unit_proj[:, K : 2 * K], preferred_element_type=jnp.float32),
            jnp.dot(hidden, unit_proj[:, 2 * K :], preferred_element_type=jnp.float32),
        ],
        axis=1,
    )
    unit_side = lax.psum(unit_part, ("tensor", "dp"))
    in_side = jnp.concatenate([feat_side[:, : 2 * K], unit_side[:, 2 * K :]], axis=1)
    out_side = jnp.concatenate([unit_side[:, : 2 * K], feat_side[:, 2 * K :]], axis=1)
    sketch = form_sketch(in_side, out_side)
    return jnp.einsum("wrc,wsc->wsr", precond, sketch, precision=lax.Precision.HIGHEST)


def solution(mesh):
    in_specs = (
        P(("groups", "dp"), "tensor"),
        P(("groups", "dp"), "tensor"),
        P(None, ("tensor", "dp"), None),
        P(("tensor", "dp"), None),
        P("tensor", None),
        P(("tensor", "dp"), None),
        P(None, ("tensor", "dp"), None),
    )
    out_specs = P(None, "groups", ("tensor", "dp"))
    return jax.shard_map(local, mesh=mesh, in_specs=in_specs, out_specs=out_specs, check_vma=False)
```

profile of v0, /device:TPU:0, one launch (start us, length us, event | category | flops | bytes accessed | tf_op | source)
XLA Modules:
  0.0 386.8 jit_solution(336281864798562320)
XLA Ops:
  6.5 0.0 all-gather.4.cloned.1.call-start
  6.5 2.3 pad_maximum_fusion
  8.8 0.0 all-gather.4.cloned.1.call-update
  8.8 0.0 all-gather.6.cloned.1.call-start
  8.9 83.6 %all-gather.4.cloned.1.call-done = bf16[2,512,2048]{2,1,0:T(8,128)(2,1)} async-done(((bf16[2,128,2048]{2,1,0:T(8,128)(2,1)}), bf16[2,512,2048]{2,1,0:T(8,128)(2,1)}) %all-gather.4.cloned.1.call-update) | async-done | bytes 4194320 | tf_op jit(solution)/shard_map/all_gather | solution.py:38
  92.4 0.0 all-gather.6.cloned.1.call-update
  92.5 0.0 all-gather.8.cloned.1.call-start
  92.5 0.7 all-gather.8.cloned.1.call-update
  93.2 0.0 all-reduce.2.cloned.1.call-start
  93.3 105.2 %all-gather.6.cloned.1.call-done = bf16[2,512,8192]{2,1,0:T(8,128)(2,1)} async-done(((bf16[2,512,2048]{2,1,0:T(8,128)(2,1)}), bf16[2,512,8192]{2,1,0:T(8,128)(2,1)}) %all-gather.6.cloned.1.call-update) | async-done | bytes 16777232 | tf_op jit(solution)/shard_map/all_gather | solution.py:44
  198.5 0.0 copy-start
  198.5 38.6 %fusion = f32[512,3584]{1,0:T(8,128)} fusion(bf16[3584,8192]{1,0:T(8,128)(2,1)} %bitcast.23, bf16[2,512,8192]{2,1,0:T(8,128)(2,1)} %all-gather.6.cloned.1.call-done), kind=kOutput, calls=%fused_computation.2 | convolution fusion | flops 30064771072 | bytes 74448896 | tf_op jit(solution)/shard_map/dot_general | solution.py:46
  237.1 0.0 copy-done
  237.1 4.3 %fusion.7 = f32[512,64]{0,1:T(8,128)S(1)} fusion(f32[512,3584]{1,0:T(8,128)} %fusion, bf16[1792,192]{0,1:T(8,128)(2,1)S(1)} %copy-done), kind=kOutput, calls=%fused_computation.13 | convolution fusion | flops 122945536 | bytes 7700480 | tf_op jit(solution)/shard_map/dot_general | solution.py:67
  241.3 22.9 %fusion.3 = f32[512,1792]{1,0:T(8,128)} fusion(bf16[1792,8192]{1,0:T(8,128)(2,1)} %param.10, bf16[2,512,8192]{2,1,0:T(8,128)(2,1)} %all-gather.6.cloned.1.call-done), kind=kOutput, calls=%fused_computation.5 | convolution fusion | flops 15032385536 | bytes 41418752 | tf_op jit(solution)/shard_map/dot_general | solution.py:47
  264.3 0.0 copy-start.1
  264.3 0.0 copy-start.2
  264.3 4.4 %fusion.6 = f32[512,64]{0,1:T(8,128)S(1)} fusion(f32[512,1792]{1,0:T(8,128)} %fusion.3, f32[512,3584]{1,0:T(8,128)} %fusion, bf16[1792,192]{0,1:T(8,128)(2,1)S(1)} %copy-done), kind=kOutput, calls=%fused_computation.12 | convolution fusion | flops 122945536 | bytes 7700480 | tf_op jit(solution)/shard_map/dot_general | solution.py:66
  268.7 0.8 copy-done.1
  269.5 1.0 copy-done.2
  270.5 1.6 fusion.8
  272.1 0.8 pad_maximum_fusion.1
  272.9 0.0 all-reduce.2.cloned.1.call-update
  272.9 0.0 all-gather.8.cloned.1.call-done
  272.9 6.9 %fusion.1 = f32[512,128]{0,1:T(8,128)S(1)} fusion(bf16[2,512,8192]{2,1,0:T(8,128)(2,1)} %all-gather.6.cloned.1.call-done, bf16[8192,192]{0,1:T(8,128)(2,1)} %all-gather.8.cloned.1.call-done), kind=kOutput, calls=%fused_computation.3 | convolution fusion | flops 1073741824 | bytes 10747904 | tf_op jit(solution)/shard_map/dot_general | solution.py:14
  279.8 6.3 %fusion.2 = f32[512,64]{0,1:T(8,128)S(1)} fusion(bf16[2,512,8192]{2,1,0:T(8,128)(2,1)} %all-gather.6.cloned.1.call-done, bf16[8192,192]{0,1:T(8,128)(2,1)} %all-gather.8.cloned.1.call-done), kind=kOutput, calls=%fused_computation.4 | convolution fusion | flops 536870912 | bytes 9568256 | tf_op jit(solution)/shard_map/dot_general | solution.py:15
  286.1 77.3 %all-reduce.2.cloned.1.call-done = f32[512,192]{0,1:T(8,128)} async-done(((f32[512,192]{0,1:T(8,128)}), f32[512,192]{0,1:T(8,128)}) %all-reduce.2.cloned.1.call-update) | async-done | bytes 393232 | tf_op jit(solution)/shard_map/psum | solution.py:71
  363.4 0.9 slice.51
  364.4 0.1 reshape.13
  364.5 1.0 slice.52
  365.5 0.1 reshape.14
  365.7 0.8 convolution_multiply_fusion
  366.4 0.2 reshape.15
  366.6 13.6 %fusion.20 = f32[3,4,256]{2,1,0:T(4,128)} fusion(f32[3,4,4096]{2,1,0:T(4,128)S(1)} %reshape.15, f32[3,256,4096]{2,1,0:T(8,128)} %param.13), kind=kOutput, calls=%fused_computation.29 | convolution fusion | flops 150994944 | bytes 12791808 | tf_op jit(solution)/shard_map/wrc,wsc->wsr/dot_general | solution.py:75
  (2 shorter events, 0.1 us)
Async XLA Ops:
  6.5 85.9 %all-gather.4.cloned.1.call-start = ((), (), s32[]{:S(2)}) async-start(), calls=%async_computation | async-start | bytes 5242880 | tf_op jit(solution)/shard_map/all_gather | solution.py:38
  8.8 189.7 %all-gather.6.cloned.1.call-start = ((), (), s32[]{:S(2)}) async-start(), calls=%async_computation.1 | async-start | bytes 20971520 | tf_op jit(solution)/shard_map/all_gather | solution.py:44
  92.5 180.4 %all-gather.8.cloned.1.call-start = ((), (), s32[]{:S(2)}) async-start(), calls=%async_computation.2 | async-start | bytes 3932160 | tf_op jit(solution)/shard_map/all_gather | solution.py:36
  93.2 270.2 %all-reduce.2.cloned.1.call-start = ((), (), s32[]{:S(2)}) async-start(), calls=%async_computation.3 | async-start | bytes 786432 | tf_op jit(solution)/shard_map/psum | solution.py:71
  198.5 38.6 %copy-start = (bf16[1792,192]{0,1:T(8,128)(2,1)S(1)}, bf16[1792,192]{0,1:T(8,128)(2,1)}, u32[]{:S(2)}) copy-start(bf16[1792,192]{0,1:T(8,128)(2,1)} %param.12) | copy-start | bytes 2064388
  264.3 5.2 %copy-start.1 = (f32[512,3584]{1,0:T(8,128)S(1)}, f32[512,3584]{1,0:T(8,128)}, u32[]{:S(2)}) copy-start(f32[512,3584]{1,0:T(8,128)} %fusion) | copy-start | bytes 22020100
  264.3 6.3 %copy-start.2 = (f32[512,1792]{1,0:T(8,128)S(1)}, f32[512,1792]{1,0:T(8,128)}, u32[]{:S(2)}) copy-start(f32[512,1792]{1,0:T(8,128)} %fusion.3) | copy-start | bytes 11010052
Sparse Core Ops, SparseCore 0:
  9.0 83.4 all-gather.3
  94.0 104.4 all-gather.5
  200.1 28.5 all-gather.7
  273.0 90.3 all-reduce.1
where the time goes:
time: 387 us
  waiting for transfers between devices  267 us (69%)
  matrix products  99.3 us (26%)
  between operations  13.2 us (3%)
  local copies, waits for them, and re-layouts  4.2 us (1%)
    all_gather x1, waiting for transfers between devices, local(): pieces = lax.all_gather(rows_all, 'tensor', axis=2, tiled=True)  105 us
    all_gather x1, waiting for transfers between devices, local(): rows_all = lax.all_gather(paired, 'dp', axis=1, tiled=True)  83.6 us
    psum x1, waiting for transfers between devices, local(): unit_side = lax.psum(unit_part, ('tensor', 'dp'))  77.3 us
    dot_general x1, matrix products, local(): lax.dot_general(pieces[0], w_both, contract_last, preferred_element_type=...  38.6 us
    dot_general x1, matrix products, local(): lax.dot_general(pieces[1], w_down, contract_last, preferred_element_type=...  22.9 us
    dot_general x1, matrix products, local(): jnp.einsum('wrc,wsc->wsr', precond, sketch, precision=lax.Precision.HIGHEST)  13.6 us
  transfers between devices with their start and end apart: 4, of which 3 were waited for; matrix products, arithmetic and copies ran while one was open for 22% of the time, Pallas kernels for 0%

commit v1 on v0

--- a/solution.py
+++ b/solution.py
@@ -68,7 +68,9 @@
         ],
         axis=1,
     )
-    unit_side = lax.psum(unit_part, ("tensor", "dp"))
+    unit_side = unit_part
+    for name in ("dp", "tensor"):
+        unit_side = lax.psum(unit_side, name)
     in_side = jnp.concatenate([feat_side[:, : 2 * K], unit_side[:, 2 * K :]], axis=1)
     out_side = jnp.concatenate([unit_side[:, : 2 * K], feat_side[:, 2 * K :]], axis=1)
     sketch = form_sketch(in_side, out_side)

time: 387 us -> 368 us (0.951)
  waiting for transfers between devices: 267 us -> 248 us
    psum x1 -> x2, waiting for transfers between devices: 77.3 us -> 58.3 us  [local(): unit_side = lax.psum(unit_side, name)]
  transfers between devices with their start and end apart: 4 -> 5, of which waited for: 3 -> 4; matrix products, arithmetic and copies ran while one was open for 22% -> 23% of each run, Pallas kernels for 0% -> 0%
where the time goes in v1:
time: 368 us
  waiting for transfers between devices  248 us (67%)
  matrix products  99.3 us (27%)
  between operations  13.2 us (4%)
  local copies, waits for them, and re-layouts  4.2 us (1%)
    all_gather x1, waiting for transfers between devices, local(): pieces = lax.all_gather(rows_all, 'tensor', axis=2, tiled=True)  105 us
    all_gather x1, waiting for transfers between devices, local(): rows_all = lax.all_gather(paired, 'dp', axis=1, tiled=True)  83.6 us
    psum x2, waiting for transfers between devices, local(): unit_side = lax.psum(unit_side, name)  58.3 us
    dot_general x1, matrix products, local(): lax.dot_general(pieces[0], w_both, contract_last, preferred_element_type=...  38.6 us
    dot_general x1, matrix products, local(): lax.dot_general(pieces[1], w_down, contract_last, preferred_element_type=...  22.9 us
    dot_general x1, matrix products, local(): jnp.einsum('wrc,wsc->wsr', precond, sketch, precision=lax.Precision.HIGHEST)  13.6 us
  transfers between devices with their start and end apart: 5, of which 4 were waited for; matrix products, arithmetic and copies ran while one was open for 23% of the time, Pallas kernels for 0%

profile of v1, /device:TPU:0, one launch (start us, length us, event | category | flops | bytes accessed | tf_op | source)
XLA Modules:
  0.0 368.0 jit_solution(13681223250753104398)
XLA Ops:
  6.5 0.0 all-gather.4.cloned.1.call-start
  6.5 2.3 pad_maximum_fusion
  8.8 0.0 all-gather.4.cloned.1.call-update
  8.8 0.0 all-gather.6.cloned.1.call-start
  8.9 83.6 %all-gather.4.cloned.1.call-done = bf16[2,512,2048]{2,1,0:T(8,128)(2,1)} async-done(((bf16[2,128,2048]{2,1,0:T(8,128)(2,1)}), bf16[2,512,2048]{2,1,0:T(8,128)(2,1)}) %all-gather.4.cloned.1.call-update) | async-done | bytes 4194320 | tf_op jit(solution)/shard_map/all_gather | solution.py:38
  92.4 0.0 all-gather.6.cloned.1.call-update
  92.5 0.0 all-gather.8.cloned.1.call-start
  92.5 0.7 all-gather.8.cloned.1.call-update
  93.2 0.0 all-reduce.3.cloned.1.call-start
  93.3 105.2 %all-gather.6.cloned.1.call-done = bf16[2,512,8192]{2,1,0:T(8,128)(2,1)} async-done(((bf16[2,512,2048]{2,1,0:T(8,128)(2,1)}), bf16[2,512,8192]{2,1,0:T(8,128)(2,1)}) %all-gather.6.cloned.1.call-update) | async-done | bytes 16777232 | tf_op jit(solution)/shard_map/all_gather | solution.py:44
  198.5 0.0 copy-start
  198.5 38.6 %fusion = f32[512,3584]{1,0:T(8,128)} fusion(bf16[3584,8192]{1,0:T(8,128)(2,1)} %bitcast.23, bf16[2,512,8192]{2,1,0:T(8,128)(2,1)} %all-gather.6.cloned.1.call-done), kind=kOutput, calls=%fused_computation.2 | convolution fusion | flops 30064771072 | bytes 74448896 | tf_op jit(solution)/shard_map/dot_general | solution.py:46
  237.1 0.0 copy-done
  237.1 4.3 %fusion.7 = f32[512,64]{0,1:T(8,128)S(1)} fusion(f32[512,3584]{1,0:T(8,128)} %fusion, bf16[1792,192]{0,1:T(8,128)(2,1)S(1)} %copy-done), kind=kOutput, calls=%fused_computation.13 | convolution fusion | flops 122945536 | bytes 7700480 | tf_op jit(solution)/shard_map/dot_general | solution.py:67
  241.3 22.9 %fusion.3 = f32[512,1792]{1,0:T(8,128)} fusion(bf16[1792,8192]{1,0:T(8,128)(2,1)} %param.10, bf16[2,512,8192]{2,1,0:T(8,128)(2,1)} %all-gather.6.cloned.1.call-done), kind=kOutput, calls=%fused_computation.5 | convolution fusion | flops 15032385536 | bytes 41418752 | tf_op jit(solution)/shard_map/dot_general | solution.py:47
  264.3 0.0 copy-start.1
  264.3 0.0 copy-start.2
  264.3 4.4 %fusion.6 = f32[512,64]{0,1:T(8,128)S(1)} fusion(f32[512,1792]{1,0:T(8,128)} %fusion.3, f32[512,3584]{1,0:T(8,128)} %fusion, bf16[1792,192]{0,1:T(8,128)(2,1)S(1)} %copy-done), kind=kOutput, calls=%fused_computation.12 | convolution fusion | flops 122945536 | bytes 7700480 | tf_op jit(solution)/shard_map/dot_general | solution.py:66
  268.7 0.8 copy-done.1
  269.5 1.0 copy-done.2
  270.5 1.6 fusion.8
  272.1 0.8 pad_maximum_fusion.1
  272.9 0.0 all-reduce.3.cloned.1.call-update
  272.9 0.2 all-reduce.5.cloned.1.call-start
  273.1 0.0 all-gather.8.cloned.1.call-done
  273.1 6.9 %fusion.1 = f32[512,128]{0,1:T(8,128)S(1)} fusion(bf16[2,512,8192]{2,1,0:T(8,128)(2,1)} %all-gather.6.cloned.1.call-done, bf16[8192,192]{0,1:T(8,128)(2,1)} %all-gather.8.cloned.1.call-done), kind=kOutput, calls=%fused_computation.3 | convolution fusion | flops 1073741824 | bytes 10747904 | tf_op jit(solution)/shard_map/dot_general | solution.py:14
  280.0 30.1 %all-reduce.3.cloned.1.call-done = f32[512,192]{0,1:T(8,128)} async-done(((f32[512,192]{0,1:T(8,128)}), f32[512,192]{0,1:T(8,128)}) %all-reduce.3.cloned.1.call-update) | async-done | bytes 393232 | tf_op jit(solution)/shard_map/psum | solution.py:73
  310.1 0.0 all-reduce.5.cloned.1.call-update
  310.1 6.3 %fusion.2 = f32[512,64]{0,1:T(8,128)S(1)} fusion(bf16[2,512,8192]{2,1,0:T(8,128)(2,1)} %all-gather.6.cloned.1.call-done, bf16[8192,192]{0,1:T(8,128)(2,1)} %all-gather.8.cloned.1.call-done), kind=kOutput, calls=%fused_computation.4 | convolution fusion | flops 536870912 | bytes 9568256 | tf_op jit(solution)/shard_map/dot_general | solution.py:15
  316.4 28.3 %all-reduce.5.cloned.1.call-done = f32[512,192]{0,1:T(8,128)} async-done(((f32[512,192]{0,1:T(8,128)}), f32[512,192]{0,1:T(8,128)}) %all-reduce.5.cloned.1.call-update) | async-done | bytes 393232 | tf_op jit(solution)/shard_map/psum | solution.py:73
  344.7 0.9 slice.51
  345.6 0.1 reshape.13
  345.8 1.0 slice.52
  346.8 0.1 reshape.14
  346.9 0.7 convolution_multiply_fusion
  347.7 0.2 reshape.15
  347.9 13.6 %fusion.20 = f32[3,4,256]{2,1,0:T(4,128)} fusion(f32[3,4,4096]{2,1,0:T(4,128)S(1)} %reshape.15, f32[3,256,4096]{2,1,0:T(8,128)} %param.13), kind=kOutput, calls=%fused_computation.29 | convolution fusion | flops 150994944 | bytes 12791808 | tf_op jit(solution)/shard_map/wrc,wsc->wsr/dot_general | solution.py:77
  (2 shorter events, 0.1 us)
Async XLA Ops:
  6.5 85.9 %all-gather.4.cloned.1.call-start = ((), (), s32[]{:S(2)}) async-start(), calls=%async_computation | async-start | bytes 5242880 | tf_op jit(solution)/shard_map/all_gather | solution.py:38
  8.8 189.7 %all-gather.6.cloned.1.call-start = ((), (), s32[]{:S(2)}) async-start(), calls=%async_computation.1 | async-start | bytes 20971520 | tf_op jit(solution)/shard_map/all_gather | solution.py:44
  92.5 180.7 %all-gather.8.cloned.1.call-start = ((), (), s32[]{:S(2)}) async-start(), calls=%async_computation.2 | async-start | bytes 3932160 | tf_op jit(solution)/shard_map/all_gather | solution.py:36
  93.2 216.9 %all-reduce.3.cloned.1.call-start = ((), (), s32[]{:S(2)}) async-start(), calls=%async_computation.3 | async-start | bytes 786432 | tf_op jit(solution)/shard_map/psum | solution.py:73
  198.5 38.6 %copy-start = (bf16[1792,192]{0,1:T(8,128)(2,1)S(1)}, bf16[1792,192]{0,1:T(8,128)(2,1)}, u32[]{:S(2)}) copy-start(bf16[1792,192]{0,1:T(8,128)(2,1)} %param.12) | copy-start | bytes 2064388
  264.3 5.2 %copy-start.1 = (f32[512,3584]{1,0:T(8,128)S(1)}, f32[512,3584]{1,0:T(8,128)}, u32[]{:S(2)}) copy-start(f32[512,3584]{1,0:T(8,128)} %fusion) | copy-start | bytes 22020100
  264.3 6.3 %copy-start.2 = (f32[512,1792]{1,0:T(8,128)S(1)}, f32[512,1792]{1,0:T(8,128)}, u32[]{:S(2)}) copy-start(f32[512,1792]{1,0:T(8,128)} %fusion.3) | copy-start | bytes 11010052
  272.9 71.8 %all-reduce.5.cloned.1.call-start = ((), (), s32[]{:S(2)}) async-start(), calls=%async_computation.4 | async-start | bytes 786432 | tf_op jit(solution)/shard_map/psum | solution.py:73
Sparse Core Ops, SparseCore 0:
  9.0 83.4 all-gather.3
  94.0 104.4 all-gather.5
  200.1 28.5 all-gather.7
  273.0 37.0 all-reduce.2
  312.4 32.1 all-reduce.4
